TPU v7x, 32 devices: a whole 2x2x4 slice. The times are simulated.
32 devices in a mesh: dp: 16 (over z, y, core), mp: 2 (over x).
Axes of the slice: x: 2, y: 2, z: 4, core: 2. Of those that a mesh axis runs over, the one named last changes fastest.
Arguments:
- tokens: bfloat16 [4096, 2048], P(('dp', 'mp')), may hold values from -6 to 6
- doc_lengths: int32 [16, 6], P('dp'), may hold values from 1 to 128, 256 in all within a row
- cotangent: bfloat16 [4096, 2048], P(('dp', 'mp')), may hold values from -6 to 6
- gain_attn: float32 [2048], replicated, may hold values from 0.1 to 1.9
- gain_mlp: float32 [2048], replicated, may hold values from 0.1 to 1.9
- w_qkv: float32 [2048, 3, 2048], P('dp', None, 'mp'), may hold values from -0.1875 to 0.1875
- w_out: float32 [2048, 2048], P('mp', 'dp'), may hold values from -0.375 to 0.375
- w_gate_up: float32 [2048, 2, 5632], P('dp', None, 'mp'), may hold values from -0.125 to 0.125
- w_down: float32 [5632, 2048], P('mp', 'dp'), may hold values from -0.078125 to 0.078125
Outputs:
- block_out: bfloat16 [4096, 2048], P(('dp', 'mp'))
- input_grad: float32 [4096, 2048], P(('dp', 'mp'))
- grad_w_qkv: float32 [2048, 3, 2048], P('dp', None, 'mp')
- grad_w_out: float32 [2048, 2048], P('mp', 'dp')
- grad_w_gate_up: float32 [2048, 2, 5632], P('dp', None, 'mp')
- grad_w_down: float32 [5632, 2048], P('mp', 'dp')
- grad_gain_attn: float32 [2048], replicated
- grad_gain_mlp: float32 [2048], replicated
Inputs may be any that keep to these rules, and one draw needn't show every extreme that they name: `doc_lengths`: each packed row's 6 lengths sum to 256, and the longest of each row is exactly 128.
All inputs are finite; a program needn't handle non-finite values.
Results may differ from a plain program's by a relative error of at most 0.014.
The roundings to bfloat16 on the way count: a program that leaves them out, or rounds other values in their place, can miss the bound.
Values may be sent and summed in bfloat16 or wider, within the bound.
No kernel may reach another device: no remote copies, remote signals or barrier semaphores. Data moves between devices by JAX's collectives and lax.ppermute only.
A program may use at most 256 MiB of HBM per device.

v0:
```python
import jax
import jax.numpy as jnp
from jax import lax
from jax.sharding import PartitionSpec as P

HD = 128
EPSILON = 1e-05
MASKED = -1e30


def row_layout(lengths, row_len):
    doc_ends = jnp.cumsum(lengths)
    places = jnp.arange(row_len, dtype=jnp.int32)
    segment = jnp.sum((places[:, None] >= doc_ends[None, :]).astype(jnp.int32), axis=1)
    starts = doc_ends - lengths
    chosen = segment[:, None] == jnp.arange(lengths.shape[0], dtype=jnp.int32)[None, :]
    doc_start = jnp.sum(jnp.where(chosen, starts[None, :], 0), axis=1)
    return (segment, places - doc_start, places)


def rotary_tables(offsets, head_size):
    half_size = head_size // 2
    frequency = 10000.0 ** (-2.0 * jnp.arange(half_size, dtype=jnp.float32) / head_size)
    angles = offsets.astype(jnp.float32)[:, None] * frequency[None, :]
    return (jnp.cos(angles), jnp.sin(angles))


def rotate(field, cosine, sine_table):
    half_size = field.shape[-1] // 2
    front_half = field[..., :half_size]
    back_half = field[..., half_size:]
    cos_rows = cosine[:, None, :]
    sin_rows = sine_table[:, None, :]
    return jnp.concatenate(
        [
            front_half * cos_rows - back_half * sin_rows,
            back_half * cos_rows + front_half * sin_rows,
        ],
        axis=-1,
    )


def rotate_back(gradient, cosine, sine_table):
    half_size = gradient.shape[-1] // 2
    front_half = gradient[..., :half_size]
    back_half = gradient[..., half_size:]
    cos_rows = cosine[:, None, :]
    sin_rows = sine_table[:, None, :]
    return jnp.concatenate(
        [
            front_half * cos_rows + back_half * sin_rows,
            back_half * cos_rows - front_half * sin_rows,
        ],
        axis=-1,
    )


def norm_scale(field):
    return lax.rsqrt(jnp.mean(field * field, axis=-1, keepdims=True) + EPSILON)


def norm_back(grad_normed, field, gain_vec):
    inverse = norm_scale(field)
    normed = field * inverse
    scaled = grad_normed * gain_vec
    grad_field = inverse * (scaled - normed * jnp.mean(scaled * normed, axis=-1, keepdims=True))
    return (grad_field, jnp.sum(grad_normed * normed, axis=0))


def masked_scores(query_block, keys_rot, seg_rows, segment, place_rows, places, scale):
    raw_scores = jnp.einsum(
        "qhe,khe->hqk", query_block, keys_rot, preferred_element_type=jnp.float32
    )
    allowed = (seg_rows[:, None] == segment[None, :]) & (places[None, :] <= place_rows[:, None])
    return jnp.where(allowed[None], raw_scores * scale, MASKED)


def scatter_sum(gradient, dimension):
    total = lax.psum_scatter(
        gradient.astype(jnp.bfloat16), "dp", scatter_dimension=dimension, tiled=True
    )
    return total.astype(jnp.float32)


def on_device(tokens, doc_lengths, cotangent, gain_attn, gain_mlp, w_qkv, w_out, w_gate_up, w_down):
    local_rows = tokens.shape[0]
    row_len = local_rows * lax.axis_size("mp")
    segment, offsets, places = row_layout(doc_lengths[0], row_len)
    cosine, sine_table = rotary_tables(offsets, HD)
    scale = HD ** (-0.5)
    block_count = max(1, row_len // 512)
    block_len = row_len // block_count
    block_starts = jnp.arange(block_count, dtype=jnp.int32) * block_len
    masters = (
        w_qkv.astype(jnp.bfloat16),
        w_out.astype(jnp.bfloat16),
        w_gate_up.astype(jnp.bfloat16),
        w_down.astype(jnp.bfloat16),
    )
    w_qkv_all, w_out_all, w_gu_all, w_down_all = (
        lax.all_gather(masters[0], "dp", axis=0, tiled=True),
        lax.all_gather(masters[1], "dp", axis=1, tiled=True),
        lax.all_gather(masters[2], "dp", axis=0, tiled=True),
        lax.all_gather(masters[3], "dp", axis=1, tiled=True),
    )
    resid_in = tokens.astype(jnp.float32)
    normed_attn = (resid_in * norm_scale(resid_in) * gain_attn).astype(jnp.bfloat16)
    attn_rows = lax.all_gather(normed_attn, "mp", axis=0, tiled=True)
    projected = jnp.einsum("td,dce->cte", attn_rows, w_qkv_all, preferred_element_type=jnp.float32)
    local_dim = projected.shape[2]
    local_heads = local_dim // HD
    projected = projected.reshape(3, row_len, local_heads, HD)
    queries = rotate(projected[0], cosine, sine_table).astype(jnp.bfloat16)
    keys_rot = rotate(projected[1], cosine, sine_table).astype(jnp.bfloat16)
    values_low = projected[2].astype(jnp.bfloat16)

    def forward_block(row_start):
        scores = masked_scores(queries, keys_rot, segment, segment, places, places, scale)
        row_max = jnp.max(scores, axis=-1, keepdims=True)
        exp_scores = jnp.exp(scores - row_max)
        denominator = jnp.sum(exp_scores, axis=-1, keepdims=True)
        attn_probs = (exp_scores / denominator).astype(jnp.bfloat16)
        mixed = jnp.einsum(
            "hqk,khe->qhe", attn_probs, values_low, preferred_element_type=jnp.float32
        )
        return (mixed.astype(jnp.bfloat16), (row_max + jnp.log(denominator))[..., 0])

    mixed_blocks, log_total = lax.map(forward_block, block_starts)
    mixed_rows = mixed_blocks.reshape(row_len, local_dim)
    part_rows = mixed_rows
    attn_part = lax.psum_scatter(
        jnp.dot(part_rows, w_out_all, preferred_element_type=jnp.float32),
        "mp",
        scatter_dimension=0,
        tiled=True,
    )
    resid_mid = resid_in + attn_part
    normed_mlp = (resid_mid * norm_scale(resid_mid) * gain_mlp).astype(jnp.bfloat16)
    mlp_rows = lax.all_gather(normed_mlp, "mp", axis=0, tiled=True)
    gate_up = jnp.einsum("td,dcf->ctf", mlp_rows, w_gu_all, preferred_element_type=jnp.float32)
    gate_sig = jax.nn.sigmoid(gate_up[0])
    gate_act = gate_up[0] * gate_sig
    hidden = (gate_act * gate_up[1]).astype(jnp.bfloat16)
    part_rows = hidden
    mlp_part = lax.psum_scatter(
        jnp.dot(part_rows, w_down_all, preferred_element_type=jnp.float32).astype(jnp.bfloat16),
        "mp",
        scatter_dimension=0,
        tiled=True,
    ).astype(jnp.float32)
    block_out = (resid_mid + mlp_part).astype(jnp.bfloat16)
    w_qkv_all, w_out_all, w_gu_all, w_down_all = (
        lax.all_gather(masters[0], "dp", axis=0, tiled=True),
        lax.all_gather(masters[1], "dp", axis=1, tiled=True),
        lax.all_gather(masters[2], "dp", axis=0, tiled=True),
        lax.all_gather(masters[3], "dp", axis=1, tiled=True),
    )
    grad_rows = lax.all_gather(cotangent, "mp", axis=0, tiled=True)
    grad_down = jnp.einsum("tf,td->fd", hidden, grad_rows, preferred_element_type=jnp.float32)
    d_hidden = jnp.einsum("td,fd->tf", grad_rows, w_down_all, preferred_element_type=jnp.float32)
    d_gate = d_hidden * gate_up[1] * gate_sig * (1.0 + gate_up[0] * (1.0 - gate_sig))
    d_up = d_hidden * gate_act
    d_gate_up = jnp.stack([d_gate, d_up]).astype(jnp.bfloat16)
    grad_gate_up = jnp.einsum(
        "td,ctf->dcf", mlp_rows, d_gate_up, preferred_element_type=jnp.float32
    )
    mlp_sums = (grad_gate_up, grad_down)
    part_rows = d_gate_up
    d_normed_mlp = lax.psum_scatter(
        jnp.einsum("ctf,dcf->td", part_rows, w_gu_all, preferred_element_type=jnp.float32),
        "mp",
        scatter_dimension=0,
        tiled=True,
    )
    d_resid_norm, gain_mlp_part = norm_back(d_normed_mlp, resid_mid, gain_mlp)
    d_resid_mid = d_resid_norm + cotangent.astype(jnp.float32)
    attn_grad_rows = lax.all_gather(d_resid_mid.astype(jnp.bfloat16), "mp", axis=0, tiled=True)
    grad_out = jnp.einsum(
        "te,td->ed", mixed_rows, attn_grad_rows, preferred_element_type=jnp.float32
    )
    d_mixed = jnp.einsum("td,ed->te", attn_grad_rows, w_out_all, preferred_element_type=jnp.float32)
    d_mixed = d_mixed.astype(jnp.bfloat16).reshape(row_len, local_heads, HD)

    def backward_block(running, pieces):
        d_keys_sum, d_values_sum = running
        row_start, log_block = pieces
        scores = masked_scores(queries, keys_rot, segment, segment, places, places, scale)
        attn_probs = jnp.exp(scores - log_block[..., None])
        d_probs = jnp.einsum(
            "qhe,khe->hqk", d_mixed, values_low, preferred_element_type=jnp.float32
        )
        row_dot = jnp.sum(attn_probs * d_probs, axis=-1, keepdims=True)
        d_raw = (attn_probs * (d_probs - row_dot) * scale).astype(jnp.bfloat16)
        d_query_block = jnp.einsum(
            "hqk,khe->qhe", d_raw, keys_rot, preferred_element_type=jnp.float32
        )
        d_keys_sum = d_keys_sum + jnp.einsum(
            "hqk,qhe->khe", d_raw, queries, preferred_element_type=jnp.float32
        )
        d_values_sum = d_values_sum + jnp.einsum(
            "hqk,qhe->khe",
            attn_probs.astype(jnp.bfloat16),
            d_mixed,
            preferred_element_type=jnp.float32,
        )
        return ((d_keys_sum, d_values_sum), d_query_block)

    zero_heads = jnp.zeros((row_len, local_heads, HD), jnp.float32)
    (d_keys, d_values), d_query_blocks = lax.scan(
        backward_block, (zero_heads, zero_heads), (block_starts, log_total)
    )
    d_queries = d_query_blocks.reshape(row_len, local_heads, HD)
    d_projected = jnp.stack(
        [
            rotate_back(d_queries, cosine, sine_table),
            rotate_back(d_keys, cosine, sine_table),
            d_values,
        ]
    )
    d_projected = d_projected.astype(jnp.bfloat16).reshape(3, row_len, local_dim)
    grad_qkv = jnp.einsum("td,cte->dce", attn_rows, d_projected, preferred_element_type=jnp.float32)
    part_rows = d_projected
    d_normed_attn = lax.psum_scatter(
        jnp.einsum("cte,dce->td", part_rows, w_qkv_all, preferred_element_type=jnp.float32).astype(
            jnp.bfloat16
        ),
        "mp",
        scatter_dimension=0,
        tiled=True,
    ).astype(jnp.float32)
    d_resid_first, gain_attn_part = norm_back(d_normed_attn, resid_in, gain_attn)
    input_grad = d_resid_mid + d_resid_first
    gain_totals = lax.psum((gain_attn_part, gain_mlp_part), ("dp", "mp"))
    weight_sums = (
        scatter_sum(grad_qkv, 0),
        scatter_sum(grad_out, 1),
        scatter_sum(mlp_sums[0], 0),
        scatter_sum(mlp_sums[1], 1),
    )
    return (
        block_out,
        input_grad,
        weight_sums[0],
        weight_sums[1],
        weight_sums[2],
        weight_sums[3],
        gain_totals[0],
        gain_totals[1],
    )


def solution(mesh):
    return jax.shard_map(
        on_device,
        mesh=mesh,
        in_specs=(
            P(("dp", "mp"), None),
            P("dp", None),
            P(("dp", "mp"), None),
            P(),
            P(),
            P("dp", None, "mp"),
            P("mp", "dp"),
            P("dp", None, "mp"),
            P("mp", "dp"),
        ),
        out_specs=(
            P(("dp", "mp"), None),
            P(("dp", "mp"), None),
            P("dp", None, "mp"),
            P("mp", "dp"),
            P("dp", None, "mp"),
            P("mp", "dp"),
            P(),
            P(),
        ),
        check_vma=False,
    )
```

profile of v0, /device:TPU:0, one launch (start us, length us, event | category | flops | bytes accessed | tf_op | source)
XLA Modules:
  0.0 1241.6 jit_solution(8914130683031569904)
XLA Ops:
  7.2 1.3 fusion.33
  9.1 2.0 fusion.30
  14.1 21.2 %all-gather.9.cloned.1.call-done = bf16[256,2048]{1,0:T(8,128)(2,1)} async-done(((bf16[128,2048]{1,0:T(8,128)(2,1)}), bf16[256,2048]{1,0:T(8,128)(2,1)}) %all-gather.9.cloned.1.call-update) | async-done | bytes 1048592 | tf_op jit(solution)/shard_map/all_gather | solution.py:108
  35.3 103.2 %all-gather.11.cloned.1.call-done = bf16[2048,3,1024]{2,0,1:T(8,128)(2,1)} async-done(((bf16[128,3,1024]{2,0,1:T(8,128)(2,1)}), bf16[2048,3,1024]{2,0,1:T(8,128)(2,1)}) %all-gather.11.cloned.1.call-update) | async-done | bytes 12582928 | tf_op jit(solution)/shard_map/all_gather | solution.py:101
  138.5 6.7 convolution_bitcast_fusion.3
  149.8 42.2 %all-gather.13.cloned.1.call-done = bf16[1024,2048]{1,0:T(8,128)(2,1)} async-done(((bf16[1024,128]{1,0:T(8,128)(2,1)}), bf16[1024,2048]{1,0:T(8,128)(2,1)}) %all-gather.13.cloned.1.call-update) | async-done | bytes 4194320 | tf_op jit(solution)/shard_map/all_gather | solution.py:102
  192.0 4.8 fusion.66
  196.9 30.2 %reduce-scatter.13.cloned.1.call-done = f32[128,2048]{1,0:T(8,128)} async-done(((f32[256,2048]{1,0:T(8,128)}), f32[128,2048]{1,0:T(8,128)}) %reduce-scatter.13.cloned.1.call-update) | async-done | bytes 1048592 | tf_op jit(solution)/shard_map/reduce_scatter | solution.py:131
  227.1 1.6 multiply_reduce_fusion.3
  229.7 3.1 copy.150
  233.6 2.3 convert_element_type.123
  236.5 14.6 %all-gather.15.cloned.1.call-done = bf16[256,2048]{1,0:T(8,128)(2,1)} async-done(((bf16[128,2048]{1,0:T(8,128)(2,1)}), bf16[256,2048]{1,0:T(8,128)(2,1)}) %all-gather.15.cloned.1.call-update) | async-done | bytes 1048592 | tf_op jit(solution)/shard_map/all_gather | solution.py:139
  251.1 120.7 %all-gather.17.cloned.1.call-done = bf16[2048,2,2816]{2,0,1:T(8,128)(2,1)} async-done(((bf16[128,2,2816]{2,0,1:T(8,128)(2,1)}), bf16[2048,2,2816]{2,0,1:T(8,128)(2,1)}) %all-gather.17.cloned.1.call-update) | async-done | bytes 23068688 | tf_op jit(solution)/shard_map/all_gather | solution.py:103
  371.8 12.7 %convolution_bitcast_fusion = f32[2,256,2816]{2,1,0:T(8,128)} fusion(bf16[2048,2,2816]{2,0,1:T(8,128)(2,1)} %all-gather.17.cloned.1.call-done, bf16[256,2048]{1,0:T(8,128)(2,1)} %all-gather.15.cloned.1.call-done), kind=kOutput, calls=%fused_computation.4 | convolution fusion | flops 5905580032 | bytes 29884416 | tf_op jit(solution)/shard_map/td,dcf->ctf/dot_general | solution.py:140
  384.4 10.2 all-gather.21.cloned.1.call-done
  394.6 99.7 %all-gather.19.cloned.1.call-done = bf16[2816,2048]{1,0:T(8,128)(2,1)} async-done(((bf16[2816,128]{1,0:T(8,128)(2,1)}), bf16[2816,2048]{1,0:T(8,128)(2,1)}) %all-gather.19.cloned.1.call-update) | async-done | bytes 11534352 | tf_op jit(solution)/shard_map/all_gather | solution.py:104
  494.3 12.4 fusion.18
  506.7 12.5 %convolution_bitcast_fusion.2 = f32[256,2048]{1,0:T(8,128)} fusion(bf16[2048,2,2816]{2,0,1:T(8,128)(2,1)} %all-gather.17.cloned.1.call-done, bf16[1,256,2816]{2,1,0:T(8,128)(2,1)} %get-tuple-element.106, bf16[1,256,2816]{2,1,0:T(8,128)(2,1)} %get-tuple-element.105), kind=kOutput, calls=%fused_computation.16 | convolution fusion | flops 5907021824 | bytes 28049408 | tf_op jit(solution)/shard_map/ctf,dcf->td/dot_general | solution.py:170
  519.3 30.2 %reduce-scatter.17.cloned.1.call-done = f32[128,2048]{1,0:T(8,128)} async-done(((f32[256,2048]{1,0:T(8,128)}), f32[128,2048]{1,0:T(8,128)}) %reduce-scatter.17.cloned.1.call-update) | async-done | bytes 1048592 | tf_op jit(solution)/shard_map/reduce_scatter | solution.py:169
  549.5 1.7 multiply_reduce_fusion.1
  552.6 21.2 %all-gather.23.cloned.1.call-done = bf16[256,2048]{1,0:T(8,128)(2,1)} async-done(((bf16[128,2048]{1,0:T(8,128)(2,1)}), bf16[256,2048]{1,0:T(8,128)(2,1)}) %all-gather.23.cloned.1.call-update) | async-done | bytes 1048592 | tf_op jit(solution)/shard_map/all_gather | solution.py:177
  573.8 4.6 convolution_convert_fusion.7
  578.4 2.0 copy.133
  580.5 3.0 fusion.47
  583.5 1.3 convolution_convert_fusion.5
  584.8 4.8 fusion.19
  589.6 4.7 fusion.22
  594.3 2.1 copy.109
  596.4 2.3 add_convert_fusion.1
  601.6 9.4 fusion.2
  611.3 8.4 convolution_convert_fusion.4
  619.8 4.4 convolution_convert_fusion.3
  624.2 6.4 copy.125
  631.9 6.0 convolution_convert_fusion.1
  637.9 15.8 %copy.127 = bf16[2816,2048]{0,1:T(8,128)(2,1)} copy(bf16[2816,2048]{1,0:T(8,128)(2,1)} %convolution_convert_fusion.1) | data formatting | bytes 23068672
  655.3 7.4 convolution_convert_fusion.2
  664.5 13.2 %convolution_convert_fusion = bf16[2048,2,2816]{2,0,1:T(8,128)(2,1)} fusion(bf16[1,256,2816]{2,1,0:T(8,128)(2,1)} %get-tuple-element.106, bf16[1,256,2816]{2,1,0:T(8,128)(2,1)S(1)} %copy-done.16, bf16[256,2048]{1,0:T(8,128)(2,1)S(1)} %copy-done.3), kind=kOutput, calls=%fused_computation.1 | convolution fusion | flops 5922881536 | bytes 27000832 | tf_op jit(solution)/shard_map/td,ctf->dcf/dot_general | solution.py:164
  678.7 1.5 fusion.32
  680.2 40.9 %all-reduce = (f32[2048]{0:T(1024)}, f32[2048]{0:T(1024)}) all-reduce(f32[2048]{0:T(1024)S(1)} %get-tuple-element.99, f32[2048]{0:T(1024)S(1)} %get-tuple-element.97), channel_id=1, replica_groups=mesh['dp'=16,'mp'=2] {'dp','mp'}, use_global_device_ids=true, to_apply=%region_19.20 | all-reduce | flops 4096 | bytes 32768 | tf_op jit(solution)/shard_map/psum | solution.py:233
  721.2 2.9 fusion.28
  724.1 7.5 reduce-scatter.25.cloned.1.call-done
  733.5 128.2 %reduce-scatter.27.cloned.1.call-done = bf16[128,2816]{1,0:T(8,128)(2,1)} async-done(((bf16[2048,2816]{1,0:T(8,128)(2,1)}), bf16[128,2816]{1,0:T(8,128)(2,1)}) %reduce-scatter.27.cloned.1.call-update) | async-done | bytes 720912
  861.7 1.5 copy.128
  863.2 1.2 convert_element_type.141
  864.4 135.4 %reduce-scatter.21.cloned.1.call-done = bf16[128,3,1024]{2,0,1:T(8,128)(2,1)} async-done(((bf16[2048,3,1024]{2,0,1:T(8,128)(2,1)}), bf16[128,3,1024]{2,0,1:T(8,128)(2,1)}) %reduce-scatter.21.cloned.1.call-update) | async-done | bytes 786448 | tf_op jit(solution)/shard_map/reduce_scatter | solution.py:79
  999.8 2.5 convert_element_type.135
  1002.2 228.2 %reduce-scatter.23.cloned.1.call-done = bf16[128,2,2816]{2,0,1:T(8,128)(2,1)} async-done(((bf16[2048,2,2816]{2,0,1:T(8,128)(2,1)}), bf16[128,2,2816]{2,0,1:T(8,128)(2,1)}) %reduce-scatter.23.cloned.1.call-update) | async-done | bytes 1441808 | tf_op jit(solution)/shard_map/reduce_scatter | solution.py:79
  1230.4 4.4 copy.112
  (137 shorter events, 22.6 us)
Async XLA Ops:
  7.2 4.0 copy-start.15
  7.2 28.1 %all-gather.9.cloned.1.call-start = ((), (), s32[]{:S(2)}) async-start(), calls=%async_computation.8 | async-start | bytes 1572864 | tf_op jit(solution)/shard_map/all_gather | solution.py:108
  11.1 1.2 copy-start.20
  11.1 2.0 copy-start.33
  11.1 127.4 %all-gather.11.cloned.1.call-start = ((), (), s32[]{:S(2)}) async-start(), calls=%async_computation.9 | async-start | bytes 13369344 | tf_op jit(solution)/shard_map/all_gather | solution.py:101
  12.2 179.8 %all-gather.13.cloned.1.call-start = ((), (), s32[]{:S(2)}) async-start(), calls=%async_computation.10 | async-start | bytes 4456448 | tf_op jit(solution)/shard_map/all_gather | solution.py:102
  13.0 214.0 %reduce-scatter.13.cloned.1.call-start = ((), (), s32[]{:S(2)}) async-start(), calls=%async_computation.11 | async-start | bytes 3145728 | tf_op jit(solution)/shard_map/reduce_scatter | solution.py:131
  145.9 3.4 copy-start.10
  147.6 1.0 copy-start.12
  147.7 1.2 copy-start.13
  147.7 1.3 copy-start.14
  149.8 47.0 %copy-start.17 = (bf16[8,128,256]{2,1,0:T(8,128)(2,1)}, bf16[8,128,256]{2,1,0:T(8,128)(2,1)S(1)}, u32[]{:S(2)}) copy-start(bf16[8,128,256]{2,1,0:T(8,128)(2,1)S(1)} %convolution_convert_fusion.6) | copy-start | bytes 1572868
  196.8 31.9 %copy-start.25 = (f32[2048]{0:T(1024)S(1)}, f32[2048]{0:T(1024)}, u32[]{:S(2)}) copy-start(f32[2048]{0:T(1024)} %param.13) | copy-start | bytes 24580
  196.8 54.3 %all-gather.15.cloned.1.call-start = ((), (), s32[]{:S(2)}) async-start(), calls=%async_computation.12 | async-start | bytes 1572864 | tf_op jit(solution)/shard_map/all_gather | solution.py:139
  228.7 322.5 %copy-start.27 = (f32[128]{0:T(128)}, f32[128]{0:T(128)S(1)}, u32[]{:S(2)}) copy-start(f32[128]{0:T(128)S(1)} %add_rsqrt_fusion) | copy-start | bytes 1540
  229.7 142.1 %all-gather.17.cloned.1.call-start = ((), (), s32[]{:S(2)}) async-start(), calls=%async_computation.13 | async-start | bytes 24510464 | tf_op jit(solution)/shard_map/all_gather | solution.py:103
  232.8 161.8 %all-gather.21.cloned.1.call-start = ((), (), s32[]{:S(2)}) async-start(), calls=%async_computation.16 | async-start | bytes 1572864 | tf_op jit(solution)/shard_map/all_gather | solution.py:158
  233.6 260.7 %all-gather.19.cloned.1.call-start = ((), (), s32[]{:S(2)}) async-start(), calls=%async_computation.14 | async-start | bytes 12255232 | tf_op jit(solution)/shard_map/all_gather | solution.py:104
  235.9 313.6 %reduce-scatter.17.cloned.1.call-start = ((), (), s32[]{:S(2)}) async-start(), calls=%async_computation.17 | async-start | bytes 3145728 | tf_op jit(solution)/shard_map/reduce_scatter | solution.py:169
  519.2 54.6 %all-gather.23.cloned.1.call-start = ((), (), s32[]{:S(2)}) async-start(), calls=%async_computation.18 | async-start | bytes 1572864 | tf_op jit(solution)/shard_map/all_gather | solution.py:177
  549.5 1.7 copy-start.1
  549.5 1.7 copy-start.5
  551.2 1.2 copy-start.31
  552.4 125.4 %reduce-scatter.19.cloned.1.call-start = ((), (), s32[]{:S(2)}) async-start(), calls=%async_computation.19 | async-start | bytes 1572864 | tf_op jit(solution)/shard_map/reduce_scatter | solution.py:223
  580.5 3.0 copy-start.4
  594.3 2.1 copy-start.7
  600.5 1.0 copy-start.22
  601.6 9.4 copy-start.24
  601.6 9.7 copy-start.9
  611.0 110.2 %reduce-scatter.15.cloned.1.call-start = ((), (), s32[]{:S(2)}) async-start(), calls=%async_computation.15 | async-start | bytes 1572864 | tf_op jit(solution)/shard_map/reduce_scatter | solution.py:145
  611.3 8.5 copy-start.18
  619.8 111.8 %reduce-scatter.25.cloned.1.call-start = ((), (), s32[]{:S(2)}) async-start(), calls=%async_computation.22 | async-start | bytes 4456448
  630.7 1.2 copy-start.19
  630.7 231.0 %reduce-scatter.27.cloned.1.call-start = ((), (), s32[]{:S(2)}) async-start(), calls=%async_computation.23 | async-start | bytes 12255232
  653.7 1.2 copy-start.8
  653.7 1.4 copy-start.21
  653.7 1.5 copy-start.23
  653.7 346.0 %reduce-scatter.21.cloned.1.call-start = ((), (), s32[]{:S(2)}) async-start(), calls=%async_computation.20 | async-start | bytes 13369344 | tf_op jit(solution)/shard_map/reduce_scatter | solution.py:79
  662.6 1.2 copy-start.3
  662.6 1.8 copy-start.16
  662.7 567.7 %reduce-scatter.23.cloned.1.call-start = ((), (), s32[]{:S(2)}) async-start(), calls=%async_computation.21 | async-start | bytes 24510464 | tf_op jit(solution)/shard_map/reduce_scatter | solution.py:79
  677.7 1.1 copy-start
  677.7 1.1 copy-start.26
  677.7 1.1 copy-start.30
  677.7 43.5 %copy-start.2 = (f32[128,2048]{1,0:T(8,128)S(1)}, f32[128,2048]{1,0:T(8,128)}, u32[]{:S(2)}) copy-start(f32[128,2048]{1,0:T(8,128)} %reduce-scatter.17.cloned.1.call-done) | copy-start | bytes 3145732
  677.7 43.5 %copy-start.6 = (bf16[128,2048]{1,0:T(8,128)(2,1)S(1)}, bf16[128,2048]{1,0:T(8,128)(2,1)}, u32[]{:S(2)}) copy-start(bf16[128,2048]{1,0:T(8,128)(2,1)} %param.11) | copy-start | bytes 1572868
  677.7 43.5 %copy-start.28 = (f32[128]{0:T(128)S(1)}, f32[128]{0:T(128)}, u32[]{:S(2)}) copy-start(f32[128]{0:T(128)} %copy-done.27) | copy-start | bytes 1540
  677.7 43.5 %copy-start.32 = (f32[128]{0:T(128)S(1)}, f32[128]{0:T(128)}, u32[]{:S(2)}) copy-start(f32[128]{0:T(128)} %copy-done.31) | copy-start | bytes 1540
  (2 other events, 1.4 us)
Sparse Core Ops, SparseCore 0:
  11.3 23.9 all-gather.8
  38.1 100.4 all-gather.10
  141.3 50.7 all-gather.12
  197.0 30.0 reduce-scatter.12
  229.8 21.2 all-gather.14
  253.1 118.6 all-gather.16
  373.3 21.2 all-gather.20
  397.3 96.9 all-gather.18
  519.4 30.0 reduce-scatter.16
  552.5 21.2 all-gather.22
  611.1 20.3 reduce-scatter.18
  634.2 20.3 reduce-scatter.14
  658.5 73.0 reduce-scatter.24
  735.5 126.1 reduce-scatter.26
  865.6 134.1 reduce-scatter.20
  1003.7 226.6 reduce-scatter.22
where the time goes:
time: 1250 us; the launch traced here: 1240 us
  waiting for transfers between devices  994 us (80%)
  matrix products  118 us (9%)
  local copies, waits for them, and re-layouts  46.6 us (4%)
  blocking collectives  40.9 us (3%)
  other arithmetic  26.6 us (2%)
  between operations  14.7 us (1%)
    reduce_scatter x2, waiting for transfers between devices, scatter_sum(): lax.psum_scatter(gradient.astype(jnp.bfloat16), 'dp', scatter_dimension=d...  364 us
    unnamed x18, waiting for transfers between devices  137 us
    all_gather x1, waiting for transfers between devices, on_device(): lax.all_gather(masters[2], 'dp', axis=0, tiled=True)  121 us
    all_gather x1, waiting for transfers between devices, on_device(): lax.all_gather(masters[0], 'dp', axis=0, tiled=True)  103 us
    all_gather x1, waiting for transfers between devices, on_device(): lax.all_gather(masters[3], 'dp', axis=1, tiled=True)  99.7 us
    all_gather x1, waiting for transfers between devices, on_device(): lax.all_gather(masters[1], 'dp', axis=1, tiled=True)  42.2 us
    psum x1, blocking collectives, on_device(): gain_totals = lax.psum((gain_attn_part, gain_mlp_part), ('dp', 'mp'))  40.9 us
    unnamed x79, local copies, waits for them, and re-layouts  40.1 us
  transfers between devices with their start and end apart: 16, of which 14 were waited for; matrix products, arithmetic and copies ran while one was open for 8% of the time, Pallas kernels for 0%

commit v1 on v0

--- a/solution.py
+++ b/solution.py
@@ -6,6 +6,22 @@
 HD = 128
 EPSILON = 1e-05
 MASKED = -1e30
+
+
+def collect(x, axis, dim):
+    ways, here, hop = (lax.axis_size(axis), lax.axis_index(axis), x.shape[dim])
+    lengths = [n * ways if d == dim else n for d, n in enumerate(x.shape)]
+    full = lax.dynamic_update_slice_in_dim(jnp.zeros(lengths, x.dtype), x, here * hop, axis=dim)
+    going_up = going_down = x
+    for far in range(1, ways // 2 + 1):
+        going_up = lax.ppermute(going_up, axis, [(d, (d + 1) % ways) for d in range(ways)])
+        full = lax.dynamic_update_slice_in_dim(full, going_up, (here - far) % ways * hop, axis=dim)
+        if 2 * far < ways:
+            going_down = lax.ppermute(going_down, axis, [(d, (d - 1) % ways) for d in range(ways)])
+            full = lax.dynamic_update_slice_in_dim(
+                full, going_down, (here + far) % ways * hop, axis=dim
+            )
+    return full
 
 
 def row_layout(lengths, row_len):
@@ -100,7 +116,7 @@
     w_qkv_all, w_out_all, w_gu_all, w_down_all = (
         lax.all_gather(masters[0], "dp", axis=0, tiled=True),
         lax.all_gather(masters[1], "dp", axis=1, tiled=True),
-        lax.all_gather(masters[2], "dp", axis=0, tiled=True),
+        collect(masters[2], "dp", 0),
         lax.all_gather(masters[3], "dp", axis=1, tiled=True),
     )
     resid_in = tokens.astype(jnp.float32)

time: 1250 us -> 1360 us (1.088)
  starting transfers between devices: 1.57 us -> 196 us
  waiting for transfers between devices: 994 us -> 811 us
  local copies, waits for them, and re-layouts: 46.6 us -> 133 us
    ppermute x0 -> x15, starting transfers between devices: none -> 195 us  [the longest x8 186 us: collect(): lax.ppermute(going_up, axis, [(d, (d + 1) % ways) for d in range(ways)])]
    all_gather x1, waiting for transfers between devices: 121 us -> 0.01 us  [on_device(): lax.all_gather(masters[2], 'dp', axis=0, tiled=True)]
    all_gather x1, waiting for transfers between devices: 99.7 us -> 0.01 us  [on_device(): lax.all_gather(masters[3], 'dp', axis=1, tiled=True)]
    ppermute x0 -> x15, waiting for transfers between devices: none -> 96.6 us  [the longest x8 92.3 us: collect(): lax.ppermute(going_up, axis, [(d, (d + 1) % ways) for d in range(ways)])]
    unnamed x18, waiting for transfers between devices: 137 us -> 89.8 us
    ppermute x0 -> x15, local copies, waits for them, and re-layouts: none -> 37.9 us  [the longest x8 20.2 us: collect(): lax.ppermute(going_up, axis, [(d, (d + 1) % ways) for d in range(ways)])]
    dynamic_update_slice x0 -> x16, local copies, waits for them, and re-layouts: none -> 32.1 us  [the longest x8 21.7 us: collect(): lax.dynamic_update_slice_in_dim(full, going_up, (here - far) % ways * hop...]
    all_gather x1, waiting for transfers between devices: 21.2 us -> 0.02 us  [on_device(): lax.all_gather(d_resid_mid.astype(jnp.bfloat16), 'mp', axis=0, tiled=True)]
  transfers between devices with their start and end apart: 16 -> 31, of which waited for: 14 -> 17; matrix products, arithmetic and copies ran while one was open for 8% -> 19% of each run, Pallas kernels for 0% -> 0%
where the time goes in v1:
time: 1360 us; the launch traced here: 1350 us
  waiting for transfers between devices  811 us (60%)
  starting transfers between devices  196 us (14%)
  local copies, waits for them, and re-layouts  133 us (10%)
  matrix products  124 us (9%)
  blocking collectives  40.1 us (3%)
  other arithmetic  32.7 us (2%)
  between operations  14.7 us (1%)
    reduce_scatter x2, waiting for transfers between devices, scatter_sum(): lax.psum_scatter(gradient.astype(jnp.bfloat16), 'dp', scatter_dimension=d...  362 us
    ppermute x8, starting transfers between devices, collect(): lax.ppermute(going_up, axis, [(d, (d + 1) % ways) for d in range(ways)])  186 us
    all_gather x1, waiting for transfers between devices, on_device(): lax.all_gather(masters[0], 'dp', axis=0, tiled=True)  103 us
    ppermute x8, waiting for transfers between devices, collect(): lax.ppermute(going_up, axis, [(d, (d + 1) % ways) for d in range(ways)])  92.3 us
    unnamed x18, waiting for transfers between devices  89.8 us
    reduce_scatter x1, waiting for transfers between devices, on_device(): lax.psum_scatter(jnp.einsum('ctf,dcf->td', part_rows, w_gu_all, preferred...  47.9 us
    all_gather x1, waiting for transfers between devices, on_device(): lax.all_gather(masters[1], 'dp', axis=1, tiled=True)  42.2 us
    psum x1, blocking collectives, on_device(): gain_totals = lax.psum((gain_attn_part, gain_mlp_part), ('dp', 'mp'))  40.1 us
  transfers between devices with their start and end apart: 31, of which 17 were waited for; matrix products, arithmetic and copies ran while one was open for 19% of the time, Pallas kernels for 0%

profile of v1, /device:TPU:0, one launch (start us, length us, event | category | flops | bytes accessed | tf_op | source)
XLA Modules:
  0.0 1351.5 jit_solution(18258707386945879456)
XLA Ops:
  14.1 21.2 %all-gather.9.cloned.1.call-done = bf16[256,2048]{1,0:T(8,128)(2,1)} async-done(((bf16[128,2048]{1,0:T(8,128)(2,1)}), bf16[256,2048]{1,0:T(8,128)(2,1)}) %all-gather.9.cloned.1.call-update) | async-done | bytes 1048592 | tf_op jit(solution)/shard_map/all_gather | solution.py:124
  35.3 103.2 %all-gather.11.cloned.1.call-done = bf16[2048,3,1024]{2,0,1:T(8,128)(2,1)} async-done(((bf16[128,3,1024]{2,0,1:T(8,128)(2,1)}), bf16[2048,3,1024]{2,0,1:T(8,128)(2,1)}) %all-gather.11.cloned.1.call-update) | async-done | bytes 12582928 | tf_op jit(solution)/shard_map/all_gather | solution.py:117
  138.5 6.7 convolution_bitcast_fusion.3
  149.9 42.2 %all-gather.13.cloned.1.call-done = bf16[1024,2048]{1,0:T(8,128)(2,1)} async-done(((bf16[1024,128]{1,0:T(8,128)(2,1)}), bf16[1024,2048]{1,0:T(8,128)(2,1)}) %all-gather.13.cloned.1.call-update) | async-done | bytes 4194320 | tf_op jit(solution)/shard_map/all_gather | solution.py:118
  192.0 4.8 fusion.66
  196.9 30.2 %reduce-scatter.13.cloned.1.call-done = f32[128,2048]{1,0:T(8,128)} async-done(((f32[256,2048]{1,0:T(8,128)}), f32[128,2048]{1,0:T(8,128)}) %reduce-scatter.13.cloned.1.call-update) | async-done | bytes 1048592 | tf_op jit(solution)/shard_map/reduce_scatter | solution.py:147
  232.7 3.1 copy.233
  235.9 4.4 collective-permute-start.1
  240.3 17.0 %collective-permute-done = bf16[128,2,2816]{2,0,1:T(8,128)(2,1)S(1)} collective-permute-done((bf16[128,2,2816]{2,0,1:T(8,128)(2,1)}, bf16[128,2,2816]{2,0,1:T(8,128)(2,1)S(1)}, u32[]{:S(2)}, u32[]{:S(2)}) %collective-permute-start) | collective-permute-done | bytes 1441824 | tf_op jit(solution)/shard_map/ppermute | solution.py:17
  257.3 11.9 collective-permute-start.2
  269.2 9.3 collective-permute-done.2
  278.5 31.4 %collective-permute-start.4 = (bf16[128,2,2816]{2,0,1:T(8,128)(2,1)S(1)}, bf16[128,2,2816]{2,0,1:T(8,128)(2,1)S(1)}, u32[]{:S(2)}, u32[]{:S(2)}) collective-permute-start(bf16[128,2,2816]{2,0,1:T(8,128)(2,1)S(1)} %collective-permute-done.2), channel_id=1, source_target_pairs={{0,2},{2,4},{4,6},{6,8},{8,10},{10,12},{12,14},{14,16},{16,18},{18... | collective-permute-start | bytes 4325384 | tf_op jit(solution)/shard_map/ppermute | solution.py:17
  309.9 18.9 %collective-permute-done.4 = bf16[128,2,2816]{2,0,1:T(8,128)(2,1)S(1)} collective-permute-done((bf16[128,2,2816]{2,0,1:T(8,128)(2,1)S(1)}, bf16[128,2,2816]{2,0,1:T(8,128)(2,1)S(1)}, u32[]{:S(2)}, u32[]{:S(2)}) %collective-permute-start.4) | collective-permute-done | bytes 1441824 | tf_op jit(solution)/shard_map/ppermute | solution.py:17
  329.9 14.6 %collective-permute-start.6 = (bf16[128,2,2816]{2,0,1:T(8,128)(2,1)S(1)}, bf16[128,2,2816]{2,0,1:T(8,128)(2,1)}, u32[]{:S(2)}, u32[]{:S(2)}) collective-permute-start(bf16[128,2,2816]{2,0,1:T(8,128)(2,1)S(1)} %collective-permute-done.4), channel_id=1, source_target_pairs={{0,2},{2,4},{4,6},{6,8},{8,10},{10,12},{12,14},{14,16},{16,18},{18... | collective-permute-start | bytes 4325384 | tf_op jit(solution)/shard_map/ppermute | solution.py:17
  344.5 12.1 collective-permute-done.6
  356.6 48.8 %collective-permute-start.8 = (bf16[128,2,2816]{2,0,1:T(8,128)(2,1)}, bf16[128,2,2816]{2,0,1:T(8,128)(2,1)}, u32[]{:S(2)}, u32[]{:S(2)}) collective-permute-start(bf16[128,2,2816]{2,0,1:T(8,128)(2,1)} %collective-permute-done.6), channel_id=1, source_target_pairs={{0,2},{2,4},{4,6},{6,8},{8,10},{10,12},{12,14},{14,16},{16,18},{18... | collective-permute-start | bytes 4325384 | tf_op jit(solution)/shard_map/ppermute | solution.py:17
  407.9 8.1 broadcast_in_dim.112
  431.6 3.3 collective-permute-start.10
  443.9 4.3 collective-permute-done.9
  448.1 4.6 collective-permute-start.11
  461.8 10.3 collective-permute-done.10
  472.0 32.0 %collective-permute-start.12 = (bf16[128,2,2816]{2,0,1:T(8,128)(2,1)}, bf16[128,2,2816]{2,0,1:T(8,128)(2,1)}, u32[]{:S(2)}, u32[]{:S(2)}) collective-permute-start(bf16[128,2,2816]{2,0,1:T(8,128)(2,1)} %collective-permute-done.10), channel_id=1, source_target_pairs={{0,2},{2,4},{4,6},{6,8},{8,10},{10,12},{12,14},{14,16},{16,18},{18... | collective-permute-start | bytes 4325384 | tf_op jit(solution)/shard_map/ppermute | solution.py:17
  522.2 44.0 %collective-permute-start.14 = (bf16[128,2,2816]{2,0,1:T(8,128)(2,1)}, bf16[128,2,2816]{2,0,1:T(8,128)(2,1)}, u32[]{:S(2)}, u32[]{:S(2)}) collective-permute-start(bf16[128,2,2816]{2,0,1:T(8,128)(2,1)} %collective-permute-done.12), channel_id=1, source_target_pairs={{0,2},{2,4},{4,6},{6,8},{8,10},{10,12},{12,14},{14,16},{16,18},{18... | collective-permute-start | bytes 4325384 | tf_op jit(solution)/shard_map/ppermute | solution.py:17
  579.3 24.7 %collective-permute-done.14 = bf16[128,2,2816]{2,0,1:T(8,128)(2,1)} collective-permute-done((bf16[128,2,2816]{2,0,1:T(8,128)(2,1)}, bf16[128,2,2816]{2,0,1:T(8,128)(2,1)}, u32[]{:S(2)}, u32[]{:S(2)}) %collective-permute-start.14) | collective-permute-done | bytes 1441824 | tf_op jit(solution)/shard_map/ppermute | solution.py:17
  609.3 13.0 convolution_bitcast_fusion
  622.4 12.9 fusion.18
  635.3 12.8 convolution_bitcast_fusion.2
  648.1 47.9 %reduce-scatter.17.cloned.1.call-done = f32[128,2048]{1,0:T(8,128)} async-done(((f32[256,2048]{1,0:T(8,128)}), f32[128,2048]{1,0:T(8,128)}) %reduce-scatter.17.cloned.1.call-update) | async-done | bytes 1048592 | tf_op jit(solution)/shard_map/reduce_scatter | solution.py:185
  699.0 9.2 convolution_convert_fusion.1
  708.2 16.1 %copy.210 = bf16[2816,2048]{0,1:T(8,128)(2,1)} copy(bf16[2816,2048]{1,0:T(8,128)(2,1)} %convolution_convert_fusion.1) | data formatting | bytes 23068672
  724.9 4.6 convolution_convert_fusion.7
  731.5 3.1 fusion.47
  734.7 5.3 fusion.22
  740.0 5.5 fusion.19
  745.5 4.4 add_convert_fusion.1
  765.2 9.6 fusion.2
  775.1 8.4 convolution_convert_fusion.4
  783.6 4.4 convolution_convert_fusion.3
  788.1 6.4 copy.208
  796.1 12.5 convolution_convert_fusion
  810.3 7.6 convolution_convert_fusion.2
  818.0 33.6 %reduce-scatter.27.cloned.1.call-done = bf16[128,2816]{1,0:T(8,128)(2,1)} async-done(((bf16[2048,2816]{1,0:T(8,128)(2,1)}), bf16[128,2816]{1,0:T(8,128)(2,1)}) %reduce-scatter.27.cloned.1.call-update) | async-done | bytes 720912
  856.3 17.7 %reduce-scatter.19.cloned.1.call-done = bf16[128,2048]{1,0:T(8,128)(2,1)} async-done(((bf16[256,2048]{1,0:T(8,128)(2,1)}), bf16[128,2048]{1,0:T(8,128)(2,1)}) %reduce-scatter.19.cloned.1.call-update) | async-done | bytes 524304 | tf_op jit(solution)/shard_map/reduce_scatter | solution.py:239
  875.5 40.1 %all-reduce = (f32[2048]{0:T(1024)}, f32[2048]{0:T(1024)}) all-reduce(f32[2048]{0:T(1024)S(1)} %get-tuple-element.99, f32[2048]{0:T(1024)S(1)} %get-tuple-element.97), channel_id=1, replica_groups=mesh['dp'=16,'mp'=2] {'dp','mp'}, use_global_device_ids=true, to_apply=%region_19.20 | all-reduce | flops 4096 | bytes 32768 | tf_op jit(solution)/shard_map/psum | solution.py:249
  918.6 55.4 %reduce-scatter.25.cloned.1.call-done = bf16[128,1024]{1,0:T(8,128)(2,1)} async-done(((bf16[2048,1024]{1,0:T(8,128)(2,1)}), bf16[128,1024]{1,0:T(8,128)(2,1)}) %reduce-scatter.25.cloned.1.call-update) | async-done | bytes 262160
  975.9 228.5 %reduce-scatter.23.cloned.1.call-done = bf16[128,2,2816]{2,0,1:T(8,128)(2,1)} async-done(((bf16[2048,2,2816]{2,0,1:T(8,128)(2,1)}), bf16[128,2,2816]{2,0,1:T(8,128)(2,1)}) %reduce-scatter.23.cloned.1.call-update) | async-done | bytes 1441808 | tf_op jit(solution)/shard_map/reduce_scatter | solution.py:95
  1204.4 4.4 copy.192
  1208.8 133.4 %reduce-scatter.21.cloned.1.call-done = bf16[128,3,1024]{2,0,1:T(8,128)(2,1)} async-done(((bf16[2048,3,1024]{2,0,1:T(8,128)(2,1)}), bf16[128,3,1024]{2,0,1:T(8,128)(2,1)}) %reduce-scatter.21.cloned.1.call-update) | async-done | bytes 786448 | tf_op jit(solution)/shard_map/reduce_scatter | solution.py:95
  (218 shorter events, 128.6 us)
Async XLA Ops:
  7.2 28.1 %all-gather.9.cloned.1.call-start = ((), (), s32[]{:S(2)}) async-start(), calls=%async_computation.8 | async-start | bytes 1572864 | tf_op jit(solution)/shard_map/all_gather | solution.py:124
  11.1 127.4 %all-gather.11.cloned.1.call-start = ((), (), s32[]{:S(2)}) async-start(), calls=%async_computation.9 | async-start | bytes 13369344 | tf_op jit(solution)/shard_map/all_gather | solution.py:117
  12.2 179.8 %all-gather.13.cloned.1.call-start = ((), (), s32[]{:S(2)}) async-start(), calls=%async_computation.10 | async-start | bytes 4456448 | tf_op jit(solution)/shard_map/all_gather | solution.py:118
  13.0 214.0 %reduce-scatter.13.cloned.1.call-start = ((), (), s32[]{:S(2)}) async-start(), calls=%async_computation.11 | async-start | bytes 3145728 | tf_op jit(solution)/shard_map/reduce_scatter | solution.py:147
  149.8 47.0 %copy-start.28 = (bf16[8,128,256]{2,1,0:T(8,128)(2,1)}, bf16[8,128,256]{2,1,0:T(8,128)(2,1)S(1)}, u32[]{:S(2)}) copy-start(bf16[8,128,256]{2,1,0:T(8,128)(2,1)S(1)} %convolution_convert_fusion.6) | copy-start | bytes 1572868
  196.8 31.9 %copy-start.34 = (f32[2048]{0:T(1024)S(1)}, f32[2048]{0:T(1024)}, u32[]{:S(2)}) copy-start(f32[2048]{0:T(1024)} %param.13) | copy-start | bytes 24580
  196.8 412.5 %all-gather.15.cloned.1.call-start = ((), (), s32[]{:S(2)}) async-start(), calls=%async_computation.12 | async-start | bytes 1572864 | tf_op jit(solution)/shard_map/all_gather | solution.py:155
  228.7 469.1 %copy-start.36 = (f32[128]{0:T(128)}, f32[128]{0:T(128)S(1)}, u32[]{:S(2)}) copy-start(f32[128]{0:T(128)S(1)} %add_rsqrt_fusion) | copy-start | bytes 1540
  229.7 392.7 %all-gather.19.cloned.1.call-start = ((), (), s32[]{:S(2)}) async-start(), calls=%async_computation.15 | async-start | bytes 1572864 | tf_op jit(solution)/shard_map/all_gather | solution.py:174
  230.2 392.1 %all-gather.17.cloned.1.call-start = ((), (), s32[]{:S(2)}) async-start(), calls=%async_computation.13 | async-start | bytes 12255232 | tf_op jit(solution)/shard_map/all_gather | solution.py:120
  232.6 402.6 %all-gather.21.cloned.1.call-start = ((), (), s32[]{:S(2)}) async-start(), calls=%async_computation.16 | async-start | bytes 24510464 | tf_op jit(solution)/shard_map/all_gather | solution.py:171
  235.8 460.3 %reduce-scatter.17.cloned.1.call-start = ((), (), s32[]{:S(2)}) async-start(), calls=%async_computation.17 | async-start | bytes 3145728 | tf_op jit(solution)/shard_map/reduce_scatter | solution.py:185
  235.8 21.5 %collective-permute-start = (bf16[128,2,2816]{2,0,1:T(8,128)(2,1)}, bf16[128,2,2816]{2,0,1:T(8,128)(2,1)S(1)}, u32[]{:S(2)}, u32[]{:S(2)}) collective-permute-start(bf16[128,2,2816]{2,0,1:T(8,128)(2,1)} %copy.233), channel_id=1, source_target_pairs={{0,2},{2,4},{4,6},{6,8},{8,10},{10,12},{12,14},{14,16},{16,18},{18... | collective-permute-start | bytes 4325384 | tf_op jit(solution)/shard_map/ppermute | solution.py:17
  235.9 33.3 %collective-permute-start.1 = (bf16[128,2,2816]{2,0,1:T(8,128)(2,1)}, bf16[128,2,2816]{2,0,1:T(8,128)(2,1)S(1)}, u32[]{:S(2)}, u32[]{:S(2)}) collective-permute-start(bf16[128,2,2816]{2,0,1:T(8,128)(2,1)} %copy.233), channel_id=1, source_target_pairs={{0,30},{2,0},{4,2},{6,4},{8,6},{10,8},{12,10},{14,12},{16,14},{18,... | collective-permute-start | bytes 4325384 | tf_op jit(solution)/shard_map/ppermute | solution.py:20
  257.3 11.9 copy-start.26
  257.3 21.2 %collective-permute-start.2 = (bf16[128,2,2816]{2,0,1:T(8,128)(2,1)S(1)}, bf16[128,2,2816]{2,0,1:T(8,128)(2,1)S(1)}, u32[]{:S(2)}, u32[]{:S(2)}) collective-permute-start(bf16[128,2,2816]{2,0,1:T(8,128)(2,1)S(1)} %collective-permute-done), channel_id=1, source_target_pairs={{0,2},{2,4},{4,6},{6,8},{8,10},{10,12},{12,14},{14,16},{16,18},{18... | collective-permute-start | bytes 4325384 | tf_op jit(solution)/shard_map/ppermute | solution.py:17
  269.2 136.2 %copy-start.27 = (bf16[128,2,2816]{2,0,1:T(8,128)(2,1)}, bf16[128,2,2816]{2,0,1:T(8,128)(2,1)S(1)}, u32[]{:S(2)}) copy-start(bf16[128,2,2816]{2,0,1:T(8,128)(2,1)S(1)} %collective-permute-done.1) | copy-start | bytes 4325380
  269.2 40.8 %collective-permute-start.3 = (bf16[128,2,2816]{2,0,1:T(8,128)(2,1)S(1)}, bf16[128,2,2816]{2,0,1:T(8,128)(2,1)S(1)}, u32[]{:S(2)}, u32[]{:S(2)}) collective-permute-start(bf16[128,2,2816]{2,0,1:T(8,128)(2,1)S(1)} %collective-permute-done.1), channel_id=1, source_target_pairs={{0,30},{2,0},{4,2},{6,4},{8,6},{10,8},{12,10},{14,12},{16,14},{18,... | collective-permute-start | bytes 4325384 | tf_op jit(solution)/shard_map/ppermute | solution.py:20
  278.5 78.1 %copy-start.24 = (bf16[128,2,2816]{2,0,1:T(8,128)(2,1)}, bf16[128,2,2816]{2,0,1:T(8,128)(2,1)S(1)}, u32[]{:S(2)}) copy-start(bf16[128,2,2816]{2,0,1:T(8,128)(2,1)S(1)} %collective-permute-done.2) | copy-start | bytes 4325380
  278.5 50.2 %collective-permute-start.4 = (bf16[128,2,2816]{2,0,1:T(8,128)(2,1)S(1)}, bf16[128,2,2816]{2,0,1:T(8,128)(2,1)S(1)}, u32[]{:S(2)}, u32[]{:S(2)}) collective-permute-start(bf16[128,2,2816]{2,0,1:T(8,128)(2,1)S(1)} %collective-permute-done.2), channel_id=1, source_target_pairs={{0,2},{2,4},{4,6},{6,8},{8,10},{10,12},{12,14},{14,16},{16,18},{18... | collective-permute-start | bytes 4325384 | tf_op jit(solution)/shard_map/ppermute | solution.py:17
  309.9 95.5 %copy-start.25 = (bf16[128,2,2816]{2,0,1:T(8,128)(2,1)}, bf16[128,2,2816]{2,0,1:T(8,128)(2,1)S(1)}, u32[]{:S(2)}) copy-start(bf16[128,2,2816]{2,0,1:T(8,128)(2,1)S(1)} %collective-permute-done.3) | copy-start | bytes 4325380
  309.9 34.6 %collective-permute-start.5 = (bf16[128,2,2816]{2,0,1:T(8,128)(2,1)S(1)}, bf16[128,2,2816]{2,0,1:T(8,128)(2,1)}, u32[]{:S(2)}, u32[]{:S(2)}) collective-permute-start(bf16[128,2,2816]{2,0,1:T(8,128)(2,1)S(1)} %collective-permute-done.3), channel_id=1, source_target_pairs={{0,30},{2,0},{4,2},{6,4},{8,6},{10,8},{12,10},{14,12},{16,14},{18,... | collective-permute-start | bytes 4325384 | tf_op jit(solution)/shard_map/ppermute | solution.py:20
  329.9 26.7 %collective-permute-start.6 = (bf16[128,2,2816]{2,0,1:T(8,128)(2,1)S(1)}, bf16[128,2,2816]{2,0,1:T(8,128)(2,1)}, u32[]{:S(2)}, u32[]{:S(2)}) collective-permute-start(bf16[128,2,2816]{2,0,1:T(8,128)(2,1)S(1)} %collective-permute-done.4), channel_id=1, source_target_pairs={{0,2},{2,4},{4,6},{6,8},{8,10},{10,12},{12,14},{14,16},{16,18},{18... | collective-permute-start | bytes 4325384 | tf_op jit(solution)/shard_map/ppermute | solution.py:17
  344.5 77.9 %collective-permute-start.7 = (bf16[128,2,2816]{2,0,1:T(8,128)(2,1)}, bf16[128,2,2816]{2,0,1:T(8,128)(2,1)}, u32[]{:S(2)}, u32[]{:S(2)}) collective-permute-start(bf16[128,2,2816]{2,0,1:T(8,128)(2,1)} %collective-permute-done.5), channel_id=1, source_target_pairs={{0,30},{2,0},{4,2},{6,4},{8,6},{10,8},{12,10},{14,12},{16,14},{18,... | collective-permute-start | bytes 4325384 | tf_op jit(solution)/shard_map/ppermute | solution.py:20
  356.6 75.0 %collective-permute-start.8 = (bf16[128,2,2816]{2,0,1:T(8,128)(2,1)}, bf16[128,2,2816]{2,0,1:T(8,128)(2,1)}, u32[]{:S(2)}, u32[]{:S(2)}) collective-permute-start(bf16[128,2,2816]{2,0,1:T(8,128)(2,1)} %collective-permute-done.6), channel_id=1, source_target_pairs={{0,2},{2,4},{4,6},{6,8},{8,10},{10,12},{12,14},{14,16},{16,18},{18... | collective-permute-start | bytes 4325384 | tf_op jit(solution)/shard_map/ppermute | solution.py:17
  422.4 25.7 %collective-permute-start.9 = (bf16[128,2,2816]{2,0,1:T(8,128)(2,1)}, bf16[128,2,2816]{2,0,1:T(8,128)(2,1)}, u32[]{:S(2)}, u32[]{:S(2)}) collective-permute-start(bf16[128,2,2816]{2,0,1:T(8,128)(2,1)} %collective-permute-done.7), channel_id=1, source_target_pairs={{0,30},{2,0},{4,2},{6,4},{8,6},{10,8},{12,10},{14,12},{16,14},{18,... | collective-permute-start | bytes 4325384 | tf_op jit(solution)/shard_map/ppermute | solution.py:20
  431.6 40.5 %collective-permute-start.10 = (bf16[128,2,2816]{2,0,1:T(8,128)(2,1)}, bf16[128,2,2816]{2,0,1:T(8,128)(2,1)}, u32[]{:S(2)}, u32[]{:S(2)}) collective-permute-start(bf16[128,2,2816]{2,0,1:T(8,128)(2,1)} %collective-permute-done.8), channel_id=1, source_target_pairs={{0,2},{2,4},{4,6},{6,8},{8,10},{10,12},{12,14},{14,16},{16,18},{18... | collective-permute-start | bytes 4325384 | tf_op jit(solution)/shard_map/ppermute | solution.py:17
  443.9 11.5 copy-start.7
  448.1 64.9 %collective-permute-start.11 = (bf16[128,2,2816]{2,0,1:T(8,128)(2,1)}, bf16[128,2,2816]{2,0,1:T(8,128)(2,1)}, u32[]{:S(2)}, u32[]{:S(2)}) collective-permute-start(bf16[128,2,2816]{2,0,1:T(8,128)(2,1)} %collective-permute-done.9), channel_id=1, source_target_pairs={{0,30},{2,0},{4,2},{6,4},{8,6},{10,8},{12,10},{14,12},{16,14},{18,... | collective-permute-start | bytes 4325384 | tf_op jit(solution)/shard_map/ppermute | solution.py:20
  461.8 45.0 %copy-start.8 = (bf16[128,2,2816]{0,2,1:T(8,128)(2,1)S(1)}, bf16[128,2,2816]{0,2,1:T(8,128)(2,1)}, u32[]{:S(2)}) copy-start(bf16[128,2,2816]{0,2,1:T(8,128)(2,1)} %copy.163) | copy-start | bytes 4325380
  472.0 50.2 %collective-permute-start.12 = (bf16[128,2,2816]{2,0,1:T(8,128)(2,1)}, bf16[128,2,2816]{2,0,1:T(8,128)(2,1)}, u32[]{:S(2)}, u32[]{:S(2)}) collective-permute-start(bf16[128,2,2816]{2,0,1:T(8,128)(2,1)} %collective-permute-done.10), channel_id=1, source_target_pairs={{0,2},{2,4},{4,6},{6,8},{8,10},{10,12},{12,14},{14,16},{16,18},{18... | collective-permute-start | bytes 4325384 | tf_op jit(solution)/shard_map/ppermute | solution.py:17
  513.1 59.7 %collective-permute-start.13 = (bf16[128,2,2816]{2,0,1:T(8,128)(2,1)}, bf16[128,2,2816]{2,0,1:T(8,128)(2,1)}, u32[]{:S(2)}, u32[]{:S(2)}) collective-permute-start(bf16[128,2,2816]{2,0,1:T(8,128)(2,1)} %collective-permute-done.11), channel_id=1, source_target_pairs={{0,30},{2,0},{4,2},{6,4},{8,6},{10,8},{12,10},{14,12},{16,14},{18,... | collective-permute-start | bytes 4325384 | tf_op jit(solution)/shard_map/ppermute | solution.py:20
  522.2 46.7 %copy-start.10 = (bf16[128,2,2816]{0,2,1:T(8,128)(2,1)S(1)}, bf16[128,2,2816]{0,2,1:T(8,128)(2,1)}, u32[]{:S(2)}) copy-start(bf16[128,2,2816]{0,2,1:T(8,128)(2,1)} %copy.167) | copy-start | bytes 4325380
  522.2 81.9 %collective-permute-start.14 = (bf16[128,2,2816]{2,0,1:T(8,128)(2,1)}, bf16[128,2,2816]{2,0,1:T(8,128)(2,1)}, u32[]{:S(2)}, u32[]{:S(2)}) collective-permute-start(bf16[128,2,2816]{2,0,1:T(8,128)(2,1)} %collective-permute-done.12), channel_id=1, source_target_pairs={{0,2},{2,4},{4,6},{6,8},{8,10},{10,12},{12,14},{14,16},{16,18},{18... | collective-permute-start | bytes 4325384 | tf_op jit(solution)/shard_map/ppermute | solution.py:17
  648.1 76.8 %all-gather.23.cloned.1.call-start = ((), (), s32[]{:S(2)}) async-start(), calls=%async_computation.18 | async-start | bytes 1572864 | tf_op jit(solution)/shard_map/all_gather | solution.py:193
  699.0 152.6 %reduce-scatter.27.cloned.1.call-start = ((), (), s32[]{:S(2)}) async-start(), calls=%async_computation.23 | async-start | bytes 12255232
  724.4 149.6 %reduce-scatter.19.cloned.1.call-start = ((), (), s32[]{:S(2)}) async-start(), calls=%async_computation.19 | async-start | bytes 1572864 | tf_op jit(solution)/shard_map/reduce_scatter | solution.py:239
  774.9 140.7 %reduce-scatter.15.cloned.1.call-start = ((), (), s32[]{:S(2)}) async-start(), calls=%async_computation.14 | async-start | bytes 1572864 | tf_op jit(solution)/shard_map/reduce_scatter | solution.py:161
  783.6 190.4 %reduce-scatter.25.cloned.1.call-start = ((), (), s32[]{:S(2)}) async-start(), calls=%async_computation.22 | async-start | bytes 4456448
  794.5 409.9 %reduce-scatter.23.cloned.1.call-start = ((), (), s32[]{:S(2)}) async-start(), calls=%async_computation.21 | async-start | bytes 24510464 | tf_op jit(solution)/shard_map/reduce_scatter | solution.py:95
  808.7 533.6 %reduce-scatter.21.cloned.1.call-start = ((), (), s32[]{:S(2)}) async-start(), calls=%async_computation.20 | async-start | bytes 13369344 | tf_op jit(solution)/shard_map/reduce_scatter | solution.py:95
  817.9 56.1 %copy-start = (bf16[128,2048]{1,0:T(8,128)(2,1)S(1)}, bf16[128,2048]{1,0:T(8,128)(2,1)}, u32[]{:S(2)}) copy-start(bf16[128,2048]{1,0:T(8,128)(2,1)} %param.9) | copy-start | bytes 1572868
  817.9 56.1 %copy-start.35 = (f32[2048]{0:T(1024)S(1)}, f32[2048]{0:T(1024)}, u32[]{:S(2)}) copy-start(f32[2048]{0:T(1024)} %param.12) | copy-start | bytes 24580
  818.0 56.1 %copy-start.39 = (f32[128]{0:T(128)S(1)}, f32[128]{0:T(128)}, u32[]{:S(2)}) copy-start(f32[128]{0:T(128)} %copy-done.38) | copy-start | bytes 1540
  851.6 64.0 %copy-start.3 = (f32[128,2048]{1,0:T(8,128)S(1)}, f32[128,2048]{1,0:T(8,128)}, u32[]{:S(2)}) copy-start(f32[128,2048]{1,0:T(8,128)} %reduce-scatter.17.cloned.1.call-done) | copy-start | bytes 3145732
  851.6 64.0 %copy-start.13 = (bf16[128,2048]{1,0:T(8,128)(2,1)S(1)}, bf16[128,2048]{1,0:T(8,128)(2,1)}, u32[]{:S(2)}) copy-start(bf16[128,2048]{1,0:T(8,128)(2,1)} %param.11) | copy-start | bytes 1572868
  851.6 64.0 %copy-start.37 = (f32[128]{0:T(128)S(1)}, f32[128]{0:T(128)}, u32[]{:S(2)}) copy-start(f32[128]{0:T(128)} %copy-done.36) | copy-start | bytes 1540
  851.6 64.0 %copy-start.41 = (f32[128]{0:T(128)S(1)}, f32[128]{0:T(128)}, u32[]{:S(2)}) copy-start(f32[128]{0:T(128)} %copy-done.40) | copy-start | bytes 1540
  (26 other events, 88.1 us)
Sparse Core Ops, SparseCore 0:
  11.3 23.9 all-gather.8
  38.1 100.4 all-gather.10
  141.3 50.7 all-gather.12
  197.0 30.0 reduce-scatter.12
  229.8 21.2 all-gather.14
  252.5 21.2 all-gather.18
  276.5 152.9 all-gather.16
  431.7 199.7 all-gather.20
  648.2 47.8 reduce-scatter.16
  699.1 21.2 all-gather.22
  724.5 127.0 reduce-scatter.26
  854.3 19.6 reduce-scatter.18
  876.8 20.5 reduce-scatter.14
  901.2 72.7 reduce-scatter.24
  977.9 226.4 reduce-scatter.22
  1208.3 133.9 reduce-scatter.20
